TPU v7x, 512 devices: a whole 4x8x8 slice. The times are simulated.
512 devices in a mesh: row: 64 (over z, x, core), col: 8 (over y).
Axes of the slice: x: 4, y: 8, z: 8, core: 2. Of those that a mesh axis runs over, the one named last changes fastest.
Arguments:
- amplitudes: bfloat16 [512, 256, 256], P('col', 'row'), may hold values from -6 to 6
- integrals: bfloat16 [256, 48, 256, 256], P('row', 'col'), may hold values from -0.03125 to 0.03125
- screen: int32 [256, 48], P('row', 'col'), may hold values from -1 to 7, as said below
- owner_map: int32 [8, 8], P('col'), may hold values from 0 to 7, each once within a row
Outputs:
- ladder: float32 [512, 64, 256], P('row', 'col')
Inputs may be any that keep to these rules, and one draw needn't show every extreme that they name: `screen`: in each row and column group the 6 slots first name distinct result tiles of that group, then hold -1; at least 2 are live, and some group of some row has all 6 live.
All inputs are finite; a program needn't handle non-finite values.
Results may differ from a plain program's by a relative error of at most 0.0003.
Values may be sent and summed in bfloat16 or wider, within the bound.
A program may use at most 64 MiB of HBM per device.

v0:
```python
import jax
import jax.numpy as jnp
from jax import lax
from jax.sharding import PartitionSpec as P


def body(amplitudes, integrals, screen, owner_map):
    gathered = lax.all_gather(amplitudes, "col", axis=0, tiled=True)
    group_tiles = owner_map.shape[1]
    live_slot = screen >= 0
    labels = jnp.arange(group_tiles, dtype=jnp.int32)
    matches = screen[:, :, None] == labels[None, None, :]
    stored = jnp.sum(jnp.where(matches, owner_map[0][None, None, :], 0), axis=2)
    selector = ((stored[:, :, None] == labels[None, None, :]) & live_slot[:, :, None]).astype(
        jnp.bfloat16
    )
    placed = jnp.einsum(
        "kla,klwv->kawv", selector, integrals, preferred_element_type=jnp.float32
    ).astype(jnp.bfloat16)
    return lax.psum_scatter(
        jnp.einsum("pkw,kawv->pav", gathered, placed, preferred_element_type=jnp.float32),
        "row",
        scatter_dimension=0,
        tiled=True,
    )


def solution(mesh):
    return jax.shard_map(
        body,
        mesh=mesh,
        in_specs=(
            P("col", "row", None),
            P("row", "col", None, None),
            P("row", "col"),
            P("col", None),
        ),
        out_specs=P("row", "col", None),
        check_vma=False,
    )
```

profile of v0, /device:TPU:8, one launch (start us, length us, event | category | flops | bytes accessed | tf_op | source)
XLA Modules:
  0.0 226.7 jit_solution(1776103147567017797)
XLA Ops:
  6.5 0.0 copy-start
  6.5 0.0 all-gather.2.cloned.1.call-start
  6.5 1.7 copy.12
  8.2 0.0 all-gather.2.cloned.1.call-update
  8.3 0.0 reduce-scatter.2.cloned.1.call-start
  8.3 0.8 copy.9
  9.1 0.9 select_reduce_fusion
  10.0 0.1 copy.10
  10.1 0.7 broadcast_compare_fusion
  10.8 0.0 copy-done
  10.8 3.9 %fusion.4 = bf16[4,8,256,256]{3,1,2,0:T(8,128)(2,1)} fusion(bf16[4,6,256,256]{3,2,1,0:T(8,128)(2,1)S(1)} %copy-done, s32[4,6]{1,0:T(4,128)S(1)} %copy.10, pred[4,6]{1,0:T(4,128)(4,1)S(1)} %broadcast_compare_fusion), kind=kOutput, calls=%fused_computation.4 | convolution fusion | flops 27263360 | bytes 7340152 | tf_op jit(solution)/shard_map/kla,klwv->kawv/dot_general | solution.py:17
  14.7 39.9 %all-gather.2.cloned.1.call-done = bf16[512,4,256]{2,0,1:T(8,128)(2,1)} async-done(((bf16[64,4,256]{2,0,1:T(8,128)(2,1)}), bf16[512,4,256]{2,0,1:T(8,128)(2,1)}) %all-gather.2.cloned.1.call-update) | async-done | bytes 1048592 | tf_op jit(solution)/shard_map/all_gather | solution.py:8
  54.6 7.1 %fusion.7 = f32[512,8,256]{0,2,1:T(8,128)} fusion(bf16[4,8,256,256]{3,1,2,0:T(8,128)(2,1)} %fusion.4, bf16[512,4,256]{2,0,1:T(8,128)(2,1)} %all-gather.2.cloned.1.call-done), kind=kOutput, calls=%fused_computation.5 | convolution fusion | flops 2147483648 | bytes 9437184 | tf_op jit(solution)/shard_map/pkw,kawv->pav/dot_general | solution.py:21
  61.7 5.4 %copy.14 = f32[512,8,256]{2,1,0:T(8,128)} copy(f32[512,8,256]{0,2,1:T(8,128)} %fusion.7) | data formatting | bytes 8388608 | tf_op jit(solution)/shard_map/pkw,kawv->pav/dot_general | solution.py:21
  67.2 0.0 reduce-scatter.2.cloned.1.call-update
  67.2 152.7 %reduce-scatter.2.cloned.1.call-done = f32[8,8,256]{2,1,0:T(8,128)} async-done(((f32[512,8,256]{2,1,0:T(8,128)}), f32[8,8,256]{2,1,0:T(8,128)}) %reduce-scatter.2.cloned.1.call-update) | async-done | bytes 65552 | tf_op jit(solution)/shard_map/reduce_scatter | solution.py:20
Async XLA Ops:
  6.5 4.2 %copy-start = (bf16[4,6,256,256]{3,2,1,0:T(8,128)(2,1)S(1)}, bf16[4,6,256,256]{3,2,1,0:T(8,128)(2,1)}, u32[]{:S(2)}) copy-start(bf16[4,6,256,256]{3,2,1,0:T(8,128)(2,1)} %param.5) | copy-start | bytes 9437188
  6.5 48.1 %all-gather.2.cloned.1.call-start = ((), (), s32[]{:S(2)}) async-start(), calls=%async_computation.1 | async-start | bytes 1179648 | tf_op jit(solution)/shard_map/all_gather | solution.py:8
  8.3 211.6 %reduce-scatter.2.cloned.1.call-start = ((), (), s32[]{:S(2)}) async-start(), calls=%async_computation.2 | async-start | bytes 4259840 | tf_op jit(solution)/shard_map/reduce_scatter | solution.py:20
Sparse Core Ops, SparseCore 0:
  9.4 45.1 all-gather.1
  67.3 152.4 reduce-scatter.1
where the time goes:
time: 227 us
  waiting for transfers between devices  193 us (85%)
  between operations  13.4 us (6%)
  matrix products  11.1 us (5%)
  local copies, waits for them, and re-layouts  8.01 us (4%)
    reduce_scatter x1, waiting for transfers between devices, body(): lax.psum_scatter(jnp.einsum('pkw,kawv->pav', gathered, placed, preferred_...  153 us
    all_gather x1, waiting for transfers between devices, body(): gathered = lax.all_gather(amplitudes, 'col', axis=0, tiled=True)  39.9 us
    dot_general x1, matrix products, body(): jnp.einsum('pkw,kawv->pav', gathered, placed, preferred_element_type=jnp....  7.13 us
    dot_general x1, local copies, waits for them, and re-layouts, body(): jnp.einsum('pkw,kawv->pav', gathered, placed, preferred_element_type=jnp....  5.44 us
  transfers between devices with their start and end apart: 2, of which 2 were waited for; matrix products, arithmetic and copies ran while one was open for 3% of the time, Pallas kernels for 0%

commit v1 on v0

--- a/solution.py
+++ b/solution.py
@@ -5,7 +5,9 @@
 
 
 def body(amplitudes, integrals, screen, owner_map):
-    gathered = lax.all_gather(amplitudes, "col", axis=0, tiled=True)
+    gathered = jnp.concatenate(
+        lax.all_to_all(jnp.stack([amplitudes] * lax.axis_size("col")), "col", 0, 0), axis=0
+    )
     group_tiles = owner_map.shape[1]
     live_slot = screen >= 0
     labels = jnp.arange(group_tiles, dtype=jnp.int32)

time: 227 us -> 218 us (0.960)
  waiting for transfers between devices: 193 us -> 173 us
  starting transfers between devices: 0.04 us -> 9.92 us
    all_gather x1 -> x0, waiting for transfers between devices: 39.9 us -> none  [body(): gathered = lax.all_gather(amplitudes, 'col', axis=0, tiled=True)]
    all_to_all x0 -> x1, waiting for transfers between devices: none -> 18.6 us  [body(): lax.all_to_all(jnp.stack([amplitudes] * lax.axis_size('col')), 'col', 0, 0)]
    all_to_all x0 -> x1, starting transfers between devices: none -> 9.91 us  [body(): lax.all_to_all(jnp.stack([amplitudes] * lax.axis_size('col')), 'col', 0, 0)]
where the time goes in v1:
time: 218 us
  waiting for transfers between devices  173 us (79%)
  between operations  13.4 us (6%)
  matrix products  10.8 us (5%)
  starting transfers between devices  9.92 us (5%)
  local copies, waits for them, and re-layouts  9.83 us (5%)
    reduce_scatter x1, waiting for transfers between devices, body(): lax.psum_scatter(jnp.einsum('pkw,kawv->pav', gathered, placed, preferred_...  154 us
    all_to_all x1, waiting for transfers between devices, body(): lax.all_to_all(jnp.stack([amplitudes] * lax.axis_size('col')), 'col', 0, 0)  18.6 us
    all_to_all x1, starting transfers between devices, body(): lax.all_to_all(jnp.stack([amplitudes] * lax.axis_size('col')), 'col', 0, 0)  9.91 us
    dot_general x1, matrix products, body(): jnp.einsum('pkw,kawv->pav', gathered, placed, preferred_element_type=jnp....  6.85 us
    dot_general x1, local copies, waits for them, and re-layouts, body(): jnp.einsum('pkw,kawv->pav', gathered, placed, preferred_element_type=jnp....  5.44 us
  transfers between devices with their start and end apart: 2, of which 2 were waited for; matrix products, arithmetic and copies ran while one was open for 3% of the time, Pallas kernels for 0%

profile of v1, /device:TPU:8, one launch (start us, length us, event | category | flops | bytes accessed | tf_op | source)
XLA Modules:
  0.0 218.0 jit_solution(3774469857860281567)
XLA Ops:
  6.5 0.0 copy-start
  6.5 1.1 copy.13
  7.6 1.1 stack.2
  8.7 9.9 %all-to-all-start = ((bf16[8,64,4,256]{3,1,2,0:T(8,128)(2,1)}), bf16[8,64,4,256]{3,1,2,0:T(8,128)(2,1)}, u32[]{:S(2)}, u32[]{:S(2)}) async-start(bf16[8,64,4,256]{3,1,2,0:T(8,128)(2,1)} %stack.2), calls=%async_computation | async-start | bytes 2097152 | tf_op jit(solution)/shard_map/all_to_all | solution.py:9
  18.7 0.0 reduce-scatter.2.cloned.1.call-start
  18.7 0.8 copy.10
  19.4 0.9 select_reduce_fusion
  20.3 0.1 copy.11
  20.4 0.7 broadcast_compare_fusion
  21.1 0.0 copy-done
  21.1 3.9 %fusion.4 = bf16[4,8,256,256]{3,1,2,0:T(8,128)(2,1)} fusion(bf16[4,6,256,256]{3,2,1,0:T(8,128)(2,1)S(1)} %copy-done, s32[4,6]{1,0:T(4,128)S(1)} %copy.11, pred[4,6]{1,0:T(4,128)(4,1)S(1)} %broadcast_compare_fusion), kind=kOutput, calls=%fused_computation.4 | convolution fusion | flops 27263360 | bytes 7340152 | tf_op jit(solution)/shard_map/kla,klwv->kawv/dot_general | solution.py:19
  25.0 18.6 %all-to-all-done = bf16[8,64,4,256]{3,1,2,0:T(8,128)(2,1)} async-done(((bf16[8,64,4,256]{3,1,2,0:T(8,128)(2,1)}), bf16[8,64,4,256]{3,1,2,0:T(8,128)(2,1)}, u32[]{:S(2)}, u32[]{:S(2)}) %all-to-all-start) | async-done | bytes 1048608 | tf_op jit(solution)/shard_map/all_to_all | solution.py:9
  43.7 1.3 copy.14
  45.0 6.9 %fusion.7 = f32[512,8,256]{0,2,1:T(8,128)} fusion(bf16[512,4,256,1]{2,0,1,3:T(8,128)(2,1)S(1)} %bitcast.15, bf16[4,8,256,256]{3,1,2,0:T(8,128)(2,1)} %fusion.4), kind=kOutput, calls=%fused_computation.5 | convolution fusion | flops 2147483648 | bytes 9437184 | tf_op jit(solution)/shard_map/pkw,kawv->pav/dot_general | solution.py:23
  51.9 5.4 %copy.16 = f32[512,8,256]{2,1,0:T(8,128)} copy(f32[512,8,256]{0,2,1:T(8,128)} %fusion.7) | data formatting | bytes 8388608 | tf_op jit(solution)/shard_map/pkw,kawv->pav/dot_general | solution.py:23
  57.3 0.0 reduce-scatter.2.cloned.1.call-update
  57.3 153.9 %reduce-scatter.2.cloned.1.call-done = f32[8,8,256]{2,1,0:T(8,128)} async-done(((f32[512,8,256]{2,1,0:T(8,128)}), f32[8,8,256]{2,1,0:T(8,128)}) %reduce-scatter.2.cloned.1.call-update) | async-done | bytes 65552 | tf_op jit(solution)/shard_map/reduce_scatter | solution.py:22
Async XLA Ops:
  6.5 14.6 %copy-start = (bf16[4,6,256,256]{3,2,1,0:T(8,128)(2,1)S(1)}, bf16[4,6,256,256]{3,2,1,0:T(8,128)(2,1)}, u32[]{:S(2)}) copy-start(bf16[4,6,256,256]{3,2,1,0:T(8,128)(2,1)} %param.5) | copy-start | bytes 9437188
  8.7 34.9 %all-to-all-start = ((bf16[8,64,4,256]{3,1,2,0:T(8,128)(2,1)}), bf16[8,64,4,256]{3,1,2,0:T(8,128)(2,1)}, u32[]{:S(2)}, u32[]{:S(2)}) async-start(bf16[8,64,4,256]{3,1,2,0:T(8,128)(2,1)} %stack.2), calls=%async_computation | async-start | bytes 2097152 | tf_op jit(solution)/shard_map/all_to_all | solution.py:9
  18.7 192.5 %reduce-scatter.2.cloned.1.call-start = ((), (), s32[]{:S(2)}) async-start(), calls=%async_computation.2 | async-start | bytes 4259840 | tf_op jit(solution)/shard_map/reduce_scatter | solution.py:22
Sparse Core Ops, SparseCore 0:
  57.4 153.7 reduce-scatter.1
